TPU v7x, 256 devices: a whole 4x4x8 slice. The times are simulated.
256 devices in a mesh: ctx: 32 (over z_lo, x, y), tp: 8 (over z_hi, core).
Axes of the slice: x: 4, y: 4, z: 8 (z_hi: 4, z_lo: 2; z = z_hi * 2 + z_lo), core: 2. Of those that a mesh axis runs over, the one named last changes fastest.
Arguments:
- queries: bfloat16 [4096, 8192], P('ctx', 'tp'), may hold values from -8 to 8
- span_kv: bfloat16 [4096, 8, 2, 128], P('ctx', 'tp'), may hold values from -8 to 8
- cache_kv: bfloat16 [16384, 8, 2, 128], P('ctx', 'tp'), may hold values from -4 to 4
- out_weight: bfloat16 [8192, 8192], P('tp', 'ctx'), may hold values from -2.390625 to 2.390625
- offset: int32 [1], replicated, may hold values from 16384 to 24575
- lengths: int32 [64], replicated, may hold values from 64 to 256, as said below
Outputs:
- mixed: bfloat16 [4096, 8192], P('tp', 'ctx')
Inputs may be any that keep to these rules, and one draw needn't show every extreme that they name: `lengths`: each at most 256; in every draw some match has all 256 of its positions valid.
All inputs are finite; a program needn't handle non-finite values.
Results may differ from a plain program's by a relative error of at most 0.025.
Values may be sent and summed in bfloat16 or wider, within the bound.
A program may use at most 64 MiB of HBM per device.

v0:
```python
import math
import jax
import jax.numpy as jnp
from jax import lax
from jax.sharding import PartitionSpec as P

SLOT = 256
lowest_score = -1e30
rope_base = 500000.0


def rotate(values, positions):
    head_size = values.shape[-1]
    half_dim = head_size // 2
    frequency = jnp.exp(
        jnp.arange(half_dim, dtype=jnp.float32) * (-2.0 * math.log(rope_base) / head_size)
    )
    angles = positions.astype(jnp.float32)[:, None] * frequency[None, :]
    cosine = jnp.cos(angles)[:, None, :]
    sine_part = jnp.sin(angles)[:, None, :]
    first_half = values[..., :half_dim]
    second_half = values[..., half_dim:]
    return jnp.concatenate(
        [
            first_half * cosine - second_half * sine_part,
            second_half * cosine + first_half * sine_part,
        ],
        axis=-1,
    )


def key_block(count):
    for option in (2048, 1536, 1024, 768, 512, 384, 256, 128):
        return option
    return count


def slot_valid(cache_positions, lengths):
    match_ids = jnp.arange(lengths.shape[0], dtype=jnp.int32)
    owner = cache_positions // SLOT
    limit = jnp.sum(jnp.where(owner[:, None] == match_ids[None, :], lengths[None, :], 0), axis=1)
    return cache_positions % SLOT < limit


def online_update(carry_state, grouped, key_rows, value_rows, valid, scale):
    running_max, running_sum, accum = carry_state
    scores = (
        jnp.einsum("tkgd,nkd->tkgn", grouped, key_rows, preferred_element_type=jnp.float32) * scale
    )
    scores = jnp.where(valid, scores, lowest_score)
    new_max = jnp.maximum(running_max, jnp.max(scores, axis=-1))
    factor = jnp.exp(running_max - new_max)
    weights = jnp.where(valid, jnp.exp(scores - new_max[..., None]), 0.0)
    running_sum = running_sum * factor + jnp.sum(weights, axis=-1)
    update = jnp.einsum(
        "tkgn,nkd->tkgd",
        weights.astype(jnp.bfloat16),
        value_rows,
        preferred_element_type=jnp.float32,
    )
    accum = accum * factor[..., None] + update
    return (new_max, running_sum, accum)


def fold_blocks(carry_state, grouped, piece, mask_rule, scale):
    count = piece.shape[0]
    block = key_block(count)
    block_count = count // block
    kv_local = piece.shape[1]
    head_size = piece.shape[3]
    key_rows = piece[:, :, 0, :].reshape(block_count, block, kv_local, head_size)
    value_rows = piece[:, :, 1, :].reshape(block_count, block, kv_local, head_size)

    def advance(state_now, inputs):
        block_keys, block_values, index = inputs
        positions = index * block + jnp.arange(block, dtype=jnp.int32)
        valid = mask_rule(positions)
        return (online_update(state_now, grouped, block_keys, block_values, valid, scale), None)

    result, unused = lax.scan(
        advance, carry_state, (key_rows, value_rows, jnp.arange(block_count, dtype=jnp.int32))
    )
    return result


def body(queries, span_kv, cache_kv, out_weight, offset, lengths):
    tok_rows, width = queries.shape
    kv_local = span_kv.shape[1]
    head_size = span_kv.shape[3]
    heads_local = width // head_size
    group = heads_local // kv_local
    scale = 1.0 / math.sqrt(head_size)
    ctx_index = lax.axis_index("ctx")
    first_token = ctx_index * tok_rows
    token_ids = first_token + jnp.arange(tok_rows, dtype=jnp.int32)
    positions = offset[0] + token_ids
    rotated = rotate(
        queries.reshape(tok_rows, heads_local, head_size).astype(jnp.float32), positions
    ).astype(jnp.bfloat16)
    grouped = rotated.reshape(tok_rows, kv_local, group, head_size)
    span_keys = rotate(span_kv[:, :, 0, :].astype(jnp.float32), positions).astype(jnp.bfloat16)
    span_rotated = jnp.stack([span_keys, span_kv[:, :, 1, :]], axis=2)

    def cache_rule(key_positions):
        return slot_valid(key_positions, lengths)[None, None, None, :]

    def span_rule(key_positions):
        return (key_positions[None, :] <= token_ids[:, None])[:, None, None, :]

    start_state = (
        jnp.full((tok_rows, kv_local, group), lowest_score, jnp.float32),
        jnp.zeros((tok_rows, kv_local, group), jnp.float32),
        jnp.zeros((tok_rows, kv_local, group, head_size), jnp.float32),
    )
    state_now = fold_blocks(
        start_state, grouped, lax.all_gather(cache_kv, "ctx", axis=0, tiled=True), cache_rule, scale
    )
    state_now = fold_blocks(
        state_now,
        grouped,
        lax.all_gather(span_rotated, "ctx", axis=0, tiled=True),
        span_rule,
        scale,
    )
    attention = (state_now[2] / state_now[1][..., None]).astype(jnp.bfloat16)
    attention = attention.reshape(tok_rows, heads_local * head_size)
    projected = jnp.dot(
        lax.all_gather(attention, "ctx", axis=0, tiled=True),
        out_weight,
        preferred_element_type=jnp.float32,
    )
    return lax.psum_scatter(projected.astype(jnp.bfloat16), "tp", scatter_dimension=0, tiled=True)


def solution(mesh):
    return jax.shard_map(
        body,
        mesh=mesh,
        in_specs=(
            P("ctx", "tp"),
            P("ctx", "tp", None, None),
            P("ctx", "tp", None, None),
            P("tp", "ctx"),
            P(),
            P(),
        ),
        out_specs=P("tp", "ctx"),
        check_vma=False,
    )
```

profile of v0, /device:TPU:16, one launch (start us, length us, event | category | flops | bytes accessed | tf_op | source)
XLA Modules:
  0.0 690.7 jit_solution(2015191303401559980)
XLA Ops:
  7.3 1.0 fusion.74
  8.8 0.6 pad_maximum_fusion.1
  9.5 1.7 copy.27
  11.3 1.1 copy.28
  12.9 125.5 %all-gather.6.cloned.1.call-done = bf16[4096,1,2,128]{0,3,2,1:T(8,128)(2,1)} async-done(((bf16[128,1,2,128]{0,3,2,1:T(8,128)(2,1)}), bf16[4096,1,2,128]{0,3,2,1:T(8,128)(2,1)}) %all-gather.6.cloned.1.call-update) | async-done | bytes 2097168 | tf_op jit(solution)/shard_map/all_gather | solution.py:121
  138.4 2.7 fusion.73
  141.1 1.6 copy.34
  142.8 1.3 copy.35
  144.1 162.4 %all-gather.4.cloned.1.call-done = bf16[16384,1,2,128]{3,0,2,1:T(8,128)(2,1)} async-done(((bf16[512,1,2,128]{3,0,2,1:T(8,128)(2,1)}), bf16[16384,1,2,128]{3,0,2,1:T(8,128)(2,1)}) %all-gather.4.cloned.1.call-update) | async-done | bytes 8388624 | tf_op jit(solution)/shard_map/all_gather | solution.py:116
  306.5 5.7 fusion.72
  312.2 126.6 %while.33 = (s32[]{:T(128)}, f32[128,1,8]{0,2,1:T(8,128)S(1)}, f32[128,1,8]{0,2,1:T(8,128)S(1)}, f32[128,1,8,128]{0,3,2,1:T(8,128)S(1)}, s32[8]{0:T(128)S(1)}, /...) while((s32[]{:T(128)}, f32[128,1,8]{0,2,1:T(8,128)S(1)}, ...), condition=%wide.region_4.5_spmd.clone, body=%wide.region_0.4_spmd.clone.sunk | while | flops 1101854720 | bytes 52800976 | solution.py:80
  312.2 0.6 dynamic_slice.68
  313.6 5.6 bitcast_reduce_fusion.2
  319.2 5.2 fusion.100
  324.5 0.8 slice-done.1
  325.3 2.7 fusion.99
  328.0 0.6 dynamic_slice.68
  329.4 5.6 bitcast_reduce_fusion.2
  335.1 5.2 fusion.100
  340.3 0.8 slice-done.1
  341.1 2.7 fusion.99
  343.8 0.6 dynamic_slice.68
  345.3 5.6 bitcast_reduce_fusion.2
  350.9 5.2 fusion.100
  356.1 0.8 slice-done.1
  356.9 2.7 fusion.99
  359.7 0.6 dynamic_slice.68
  361.1 5.6 bitcast_reduce_fusion.2
  366.7 5.2 fusion.100
  372.0 0.8 slice-done.1
  372.8 2.7 fusion.99
  375.5 0.6 dynamic_slice.68
  376.9 5.6 bitcast_reduce_fusion.2
  382.5 5.2 fusion.100
  387.8 0.8 slice-done.1
  388.6 2.7 fusion.99
  391.3 0.6 dynamic_slice.68
  392.8 5.6 bitcast_reduce_fusion.2
  398.4 5.2 fusion.100
  403.6 0.8 slice-done.1
  404.4 2.7 fusion.99
  407.1 0.6 dynamic_slice.68
  408.6 5.6 bitcast_reduce_fusion.2
  414.2 5.2 fusion.100
  419.4 0.8 slice-done.1
  420.2 2.7 fusion.99
  423.0 0.6 dynamic_slice.68
  424.4 5.6 bitcast_reduce_fusion.2
  430.0 5.2 fusion.100
  435.3 0.8 slice-done.1
  436.1 2.7 fusion.99
  438.8 14.6 %while.32 = (s32[]{:T(128)}, f32[128,1,8]{0,2,1:T(8,128)S(1)}, f32[128,1,8]{0,2,1:T(8,128)S(1)}, f32[128,1,8,128]{0,3,2,1:T(8,128)S(1)}, s32[2]{0:T(128)S(1)}, /...) while((s32[]{:T(128)}, f32[128,1,8]{0,2,1:T(8,128)S(1)}, ...), condition=%wide.region_8.9_spmd.clone, body=%wide.region_5.8_spmd.clone.sunk | while | flops 1101534336 | bytes 32851120 | solution.py:80
  438.8 0.6 dynamic_slice.65
  440.4 1.4 fusion.91
  441.8 2.2 fusion.94
  444.0 2.0 fusion.93
  446.1 0.6 dynamic_slice.65
  447.7 1.4 fusion.91
  449.1 2.2 fusion.94
  451.3 2.0 fusion.93
  453.4 0.8 divide_convert_fusion
  454.4 178.3 %all-gather.8.cloned.1.call-done = bf16[4096,1024]{0,1:T(8,128)(2,1)} async-done(((bf16[128,1024]{0,1:T(8,128)(2,1)}), bf16[4096,1024]{0,1:T(8,128)(2,1)}) %all-gather.8.cloned.1.call-update) | async-done | bytes 8388624 | tf_op jit(solution)/shard_map/all_gather | solution.py:128
  632.7 7.2 %convolution_convert_fusion = bf16[4096,256]{1,0:T(8,128)(2,1)} fusion(bf16[4096,1024]{0,1:T(8,128)(2,1)} %all-gather.8.cloned.1.call-done, bf16[1024,256]{1,0:T(8,128)(2,1)S(1)} %copy-done), kind=kOutput, calls=%fused_computation.74 | convolution fusion | flops 2148532224 | bytes 11010048 | tf_op jit(solution)/shard_map/dot_general | solution.py:127
  639.9 44.3 %reduce-scatter.2.cloned.1.call-done = bf16[512,256]{1,0:T(8,128)(2,1)} async-done(((bf16[4096,256]{1,0:T(8,128)(2,1)}), bf16[512,256]{1,0:T(8,128)(2,1)}) %reduce-scatter.2.cloned.1.call-update) | async-done | bytes 262160 | tf_op jit(solution)/shard_map/reduce_scatter | solution.py:132
  (124 shorter events, 3.9 us)
Async XLA Ops:
  6.5 626.1 %copy-start = (bf16[1024,256]{1,0:T(8,128)(2,1)S(1)}, bf16[1024,256]{1,0:T(8,128)(2,1)}, u32[]{:S(2)}) copy-start(bf16[1024,256]{1,0:T(8,128)(2,1)} %param.13) | copy-start | bytes 1572868
  6.5 131.9 %all-gather.6.cloned.1.call-start = ((), (), s32[]{:S(2)}) async-start(), calls=%async_computation.2 | async-start | bytes 2162688 | tf_op jit(solution)/shard_map/all_gather | solution.py:121
  9.4 297.0 %all-gather.4.cloned.1.call-start = ((), (), s32[]{:S(2)}) async-start(), calls=%async_computation.1 | async-start | bytes 8650752 | tf_op jit(solution)/shard_map/all_gather | solution.py:116
  11.2 621.5 %all-gather.8.cloned.1.call-start = ((), (), s32[]{:S(2)}) async-start(), calls=%async_computation.3 | async-start | bytes 8650752 | tf_op jit(solution)/shard_map/all_gather | solution.py:128
  144.1 168.1 %copy-start.2 = (s32[64]{0:T(128)S(1)}, s32[64]{0:T(128)}, u32[]{:S(2)}) copy-start(s32[64]{0:T(128)} %param.15) | copy-start | bytes 772
  319.2 5.3 slice-start
  319.2 6.1 slice-start.1
  335.0 5.3 slice-start
  335.0 6.1 slice-start.1
  350.9 5.3 slice-start
  350.9 6.1 slice-start.1
  366.7 5.3 slice-start
  366.7 6.1 slice-start.1
  382.5 5.3 slice-start
  382.5 6.1 slice-start.1
  398.3 5.3 slice-start
  398.4 6.1 slice-start.1
  414.2 5.3 slice-start
  414.2 6.1 slice-start.1
  430.0 5.3 slice-start
  430.0 6.1 slice-start.1
  438.8 3.0 copy-start.1
  446.1 3.0 copy-start.1
  454.1 230.0 %reduce-scatter.2.cloned.1.call-start = ((), (), s32[]{:S(2)}) async-start(), calls=%async_computation.4 | async-start | bytes 2359296 | tf_op jit(solution)/shard_map/reduce_scatter | solution.py:132
Sparse Core Ops, SparseCore 0:
  9.6 128.8 all-gather.5
  140.2 166.1 all-gather.3
  454.3 178.3 all-gather.7
  640.0 44.1 reduce-scatter.1
where the time goes:
time: 691 us
  waiting for transfers between devices  510 us (74%)
  matrix products  101 us (15%)
  other arithmetic  29.7 us (4%)
  local copies, waits for them, and re-layouts  28 us (4%)
  between operations  14 us (2%)
  loops' own time  7.33 us (1%)
    all_gather x1, waiting for transfers between devices, body(): lax.all_gather(attention, 'ctx', axis=0, tiled=True)  178 us
    all_gather x1, waiting for transfers between devices, body(): lax.all_gather(cache_kv, 'ctx', axis=0, tiled=True)  162 us
    all_gather x1, waiting for transfers between devices, body(): lax.all_gather(span_rotated, 'ctx', axis=0, tiled=True)  125 us
    dot_general x10, matrix products, online_update(): jnp.einsum('tkgd,nkd->tkgn', grouped, key_rows, preferred_element_type=jn...  47.4 us
    dot_general x10, matrix products, online_update(): jnp.einsum('tkgn,nkd->tkgd', weights.astype(jnp.bfloat16), value_rows, pr...  46.3 us
    reduce_scatter x1, waiting for transfers between devices, body(): lax.psum_scatter(projected.astype(jnp.bfloat16), 'tp', scatter_dimension=...  44.3 us
    reduce_sum x10, other arithmetic, online_update(): running_sum = running_sum * factor + jnp.sum(weights, axis=-1)  25.3 us
  transfers between devices with their start and end apart: 4, of which 4 were waited for; matrix products, arithmetic and copies ran while one was open for 1% of the time, Pallas kernels for 0%

commit v1 on v0

--- a/solution.py
+++ b/solution.py
@@ -115,12 +115,17 @@
     state_now = fold_blocks(
         start_state, grouped, lax.all_gather(cache_kv, "ctx", axis=0, tiled=True), cache_rule, scale
     )
+    push_orders_now = lambda mine, named_axis: jnp.concatenate(
+        jax.lax.all_to_all(
+            jnp.stack([mine for _ in range(jax.lax.axis_size(named_axis))]),
+            axis_name=named_axis,
+            split_axis=0,
+            concat_axis=0,
+        ),
+        axis=0,
+    )
     state_now = fold_blocks(
-        state_now,
-        grouped,
-        lax.all_gather(span_rotated, "ctx", axis=0, tiled=True),
-        span_rule,
-        scale,
+        state_now, grouped, push_orders_now(span_rotated, "ctx"), span_rule, scale
     )
     attention = (state_now[2] / state_now[1][..., None]).astype(jnp.bfloat16)
     attention = attention.reshape(tok_rows, heads_local * head_size)

time: 691 us -> 582 us (0.84)
  waiting for transfers between devices: 510 us -> 395 us
  starting transfers between devices: 0.31 us -> 9.04 us
    all_gather x1 -> x0, waiting for transfers between devices: 125 us -> none  [body(): lax.all_gather(span_rotated, 'ctx', axis=0, tiled=True)]
    all_to_all x0 -> x1, waiting for transfers between devices: none -> 29.3 us  [body(): jax.lax.all_to_all(jnp.stack([mine for _ in range(jax.lax.axis_size(named...]
    all_gather x1, waiting for transfers between devices: 162 us -> 146 us  [body(): lax.all_gather(cache_kv, 'ctx', axis=0, tiled=True)]
    all_to_all x0 -> x1, starting transfers between devices: none -> 8.77 us  [body(): jax.lax.all_to_all(jnp.stack([mine for _ in range(jax.lax.axis_size(named...]
where the time goes in v1:
time: 582 us; the launch traced here: 581 us
  waiting for transfers between devices  395 us (68%)
  matrix products  101 us (17%)
  other arithmetic  29.1 us (5%)
  local copies, waits for them, and re-layouts  25.6 us (4%)
  between operations  13.9 us (2%)
  starting transfers between devices  9.04 us (2%)
  loops' own time  7.33 us (1%)
    all_gather x1, waiting for transfers between devices, body(): lax.all_gather(attention, 'ctx', axis=0, tiled=True)  175 us
    all_gather x1, waiting for transfers between devices, body(): lax.all_gather(cache_kv, 'ctx', axis=0, tiled=True)  146 us
    dot_general x10, matrix products, online_update(): jnp.einsum('tkgd,nkd->tkgn', grouped, key_rows, preferred_element_type=jn...  47.4 us
    dot_general x10, matrix products, online_update(): jnp.einsum('tkgn,nkd->tkgd', weights.astype(jnp.bfloat16), value_rows, pr...  46.3 us
    reduce_scatter x1, waiting for transfers between devices, body(): lax.psum_scatter(projected.astype(jnp.bfloat16), 'tp', scatter_dimension=...  43.9 us
    all_to_all x1, waiting for transfers between devices, body(): jax.lax.all_to_all(jnp.stack([mine for _ in range(jax.lax.axis_size(named...  29.3 us
    reduce_sum x10, other arithmetic, online_update(): running_sum = running_sum * factor + jnp.sum(weights, axis=-1)  25.3 us
  transfers between devices with their start and end apart: 4, of which 4 were waited for; matrix products, arithmetic and copies ran while one was open for 1% of the time, Pallas kernels for 0%

profile of v1, /device:TPU:16, one launch (start us, length us, event | category | flops | bytes accessed | tf_op | source)
XLA Modules:
  0.0 580.6 jit_solution(6810668281393273272)
XLA Ops:
  6.5 1.7 copy.41
  9.0 1.0 fusion.74
  10.6 1.9 stack.8
  12.5 8.8 %all-to-all-start = ((bf16[32,128,1,2,128]{4,1,3,2,0:T(8,128)(2,1)}), bf16[32,128,1,2,128]{4,1,3,2,0:T(8,128)(2,1)S(1)}, u32[]{:S(2)}, u32[]{:S(2)}) async-start(bf16[32,128,1,2,128]{4,1,3,2,0:T(8,128)(2,1)} %stack.8), calls=%async_computation | async-start | bytes 4194304 | tf_op jit(solution)/shard_map/all_to_all | solution.py:119
  21.4 1.1 copy.42
  23.0 29.3 %all-to-all-done = bf16[32,128,1,2,128]{4,1,3,2,0:T(8,128)(2,1)S(1)} async-done(((bf16[32,128,1,2,128]{4,1,3,2,0:T(8,128)(2,1)}), bf16[32,128,1,2,128]{4,1,3,2,0:T(8,128)(2,1)S(1)}, u32[]{:S(2)}, u32[]{:S(2)}) %all-to-all-start) | async-done | bytes 2097184 | tf_op jit(solution)/shard_map/all_to_all | solution.py:119
  52.5 1.1 fusion.73
  53.6 146.2 %all-gather.3.cloned.1.call-done = bf16[16384,1,2,128]{3,0,2,1:T(8,128)(2,1)} async-done(((bf16[512,1,2,128]{3,0,2,1:T(8,128)(2,1)}), bf16[16384,1,2,128]{3,0,2,1:T(8,128)(2,1)}) %all-gather.3.cloned.1.call-update) | async-done | bytes 8388624 | tf_op jit(solution)/shard_map/all_gather | solution.py:116
  199.8 5.7 fusion.72
  205.6 126.6 %while.33 = (s32[]{:T(128)}, f32[128,1,8]{0,2,1:T(8,128)S(1)}, f32[128,1,8]{0,2,1:T(8,128)S(1)}, f32[128,1,8,128]{0,3,2,1:T(8,128)S(1)}, s32[8]{0:T(128)S(1)}, /...) while((s32[]{:T(128)}, f32[128,1,8]{0,2,1:T(8,128)S(1)}, ...), condition=%wide.region_4.5_spmd.clone, body=%wide.region_0.4_spmd.clone.sunk | while | flops 1101854720 | bytes 52800976 | solution.py:80
  205.6 0.6 dynamic_slice.68
  207.0 5.6 bitcast_reduce_fusion.2
  212.6 5.2 fusion.100
  217.9 0.8 slice-done.1
  218.7 2.7 fusion.99
  221.4 0.6 dynamic_slice.68
  222.8 5.6 bitcast_reduce_fusion.2
  228.4 5.2 fusion.100
  233.7 0.8 slice-done.1
  234.5 2.7 fusion.99
  237.2 0.6 dynamic_slice.68
  238.7 5.6 bitcast_reduce_fusion.2
  244.3 5.2 fusion.100
  249.5 0.8 slice-done.1
  250.3 2.7 fusion.99
  253.0 0.6 dynamic_slice.68
  254.5 5.6 bitcast_reduce_fusion.2
  260.1 5.2 fusion.100
  265.4 0.8 slice-done.1
  266.2 2.7 fusion.99
  268.9 0.6 dynamic_slice.68
  270.3 5.6 bitcast_reduce_fusion.2
  275.9 5.2 fusion.100
  281.2 0.8 slice-done.1
  282.0 2.7 fusion.99
  284.7 0.6 dynamic_slice.68
  286.1 5.6 bitcast_reduce_fusion.2
  291.8 5.2 fusion.100
  297.0 0.8 slice-done.1
  297.8 2.7 fusion.99
  300.5 0.6 dynamic_slice.68
  302.0 5.6 bitcast_reduce_fusion.2
  307.6 5.2 fusion.100
  312.8 0.8 slice-done.1
  313.6 2.7 fusion.99
  316.4 0.6 dynamic_slice.68
  317.8 5.6 bitcast_reduce_fusion.2
  323.4 5.2 fusion.100
  328.7 0.8 slice-done.1
  329.5 2.7 fusion.99
  332.2 14.5 %while.32 = (s32[]{:T(128)}, f32[128,1,8]{0,2,1:T(8,128)S(1)}, f32[128,1,8]{0,2,1:T(8,128)S(1)}, f32[128,1,8,128]{0,3,2,1:T(8,128)S(1)}, s32[2]{0:T(128)S(1)}, /...) while((s32[]{:T(128)}, f32[128,1,8]{0,2,1:T(8,128)S(1)}, ...), condition=%wide.region_8.9_spmd.clone, body=%wide.region_5.8_spmd.clone.sunk | while | flops 1101534336 | bytes 32851120 | solution.py:80
  332.2 0.6 dynamic_slice.65
  333.5 0.3 broadcast_compare_fusion.2
  333.8 1.4 fusion.91
  335.2 2.2 fusion.94
  337.4 2.0 fusion.93
  339.5 0.6 dynamic_slice.65
  341.1 1.4 fusion.91
  342.5 2.2 fusion.94
  344.7 2.0 fusion.93
  346.7 0.8 divide_convert_fusion
  347.8 175.1 %all-gather.5.cloned.1.call-done = bf16[4096,1024]{0,1:T(8,128)(2,1)} async-done(((bf16[128,1024]{0,1:T(8,128)(2,1)}), bf16[4096,1024]{0,1:T(8,128)(2,1)}) %all-gather.5.cloned.1.call-update) | async-done | bytes 8388624 | tf_op jit(solution)/shard_map/all_gather | solution.py:133
  522.9 7.2 %convolution_convert_fusion = bf16[4096,256]{1,0:T(8,128)(2,1)} fusion(bf16[4096,1024]{0,1:T(8,128)(2,1)} %all-gather.5.cloned.1.call-done, bf16[1024,256]{1,0:T(8,128)(2,1)S(1)} %copy-done), kind=kOutput, calls=%fused_computation.74 | convolution fusion | flops 2148532224 | bytes 11010048 | tf_op jit(solution)/shard_map/dot_general | solution.py:132
  530.1 43.9 %reduce-scatter.2.cloned.1.call-done = bf16[512,256]{1,0:T(8,128)(2,1)} async-done(((bf16[4096,256]{1,0:T(8,128)(2,1)}), bf16[512,256]{1,0:T(8,128)(2,1)}) %reduce-scatter.2.cloned.1.call-update) | async-done | bytes 262160 | tf_op jit(solution)/shard_map/reduce_scatter | solution.py:137
  (126 shorter events, 3.7 us)
Async XLA Ops:
  6.5 516.3 %copy-start = (bf16[1024,256]{1,0:T(8,128)(2,1)S(1)}, bf16[1024,256]{1,0:T(8,128)(2,1)}, u32[]{:S(2)}) copy-start(bf16[1024,256]{1,0:T(8,128)(2,1)} %param.13) | copy-start | bytes 1572868
  6.5 193.3 %all-gather.3.cloned.1.call-start = ((), (), s32[]{:S(2)}) async-start(), calls=%async_computation.2 | async-start | bytes 8650752 | tf_op jit(solution)/shard_map/all_gather | solution.py:116
  12.5 39.8 %all-to-all-start = ((bf16[32,128,1,2,128]{4,1,3,2,0:T(8,128)(2,1)}), bf16[32,128,1,2,128]{4,1,3,2,0:T(8,128)(2,1)S(1)}, u32[]{:S(2)}, u32[]{:S(2)}) async-start(bf16[32,128,1,2,128]{4,1,3,2,0:T(8,128)(2,1)} %stack.8), calls=%async_computation | async-start | bytes 4194304 | tf_op jit(solution)/shard_map/all_to_all | solution.py:119
  21.3 501.6 %all-gather.5.cloned.1.call-start = ((), (), s32[]{:S(2)}) async-start(), calls=%async_computation.3 | async-start | bytes 8650752 | tf_op jit(solution)/shard_map/all_gather | solution.py:133
  53.6 151.9 %copy-start.2 = (f32[128,1,8,128]{0,3,2,1:T(8,128)S(1)}, f32[128,1,8,128]{0,3,2,1:T(8,128)}, u32[]{:S(2)}) copy-start(f32[128,1,8,128]{0,3,2,1:T(8,128)} %custom-call.2) | copy-start | bytes 1572868
  53.6 151.9 %copy-start.3 = (s32[64]{0:T(128)S(1)}, s32[64]{0:T(128)}, u32[]{:S(2)}) copy-start(s32[64]{0:T(128)} %param.15) | copy-start | bytes 772
  212.6 5.3 slice-start
  212.6 6.1 %slice-start.1 = ((s8[8388608]{0:T(1024)(128)(4,1)}), s8[4194304]{0:T(1024)(128)(4,1)S(1)}, s32[]{:S(2)}) async-start(s8[8388608]{0:T(1024)(128)(4,1)} %bitcast.218), calls=%async_computation.6 | async-start | bytes 8388608 | tf_op jit(solution)/shard_map/while
  228.4 5.3 slice-start
  228.4 6.1 %slice-start.1 = ((s8[8388608]{0:T(1024)(128)(4,1)}), s8[4194304]{0:T(1024)(128)(4,1)S(1)}, s32[]{:S(2)}) async-start(s8[8388608]{0:T(1024)(128)(4,1)} %bitcast.218), calls=%async_computation.6 | async-start | bytes 8388608 | tf_op jit(solution)/shard_map/while
  244.2 5.3 slice-start
  244.3 6.1 %slice-start.1 = ((s8[8388608]{0:T(1024)(128)(4,1)}), s8[4194304]{0:T(1024)(128)(4,1)S(1)}, s32[]{:S(2)}) async-start(s8[8388608]{0:T(1024)(128)(4,1)} %bitcast.218), calls=%async_computation.6 | async-start | bytes 8388608 | tf_op jit(solution)/shard_map/while
  260.1 5.3 slice-start
  260.1 6.1 %slice-start.1 = ((s8[8388608]{0:T(1024)(128)(4,1)}), s8[4194304]{0:T(1024)(128)(4,1)S(1)}, s32[]{:S(2)}) async-start(s8[8388608]{0:T(1024)(128)(4,1)} %bitcast.218), calls=%async_computation.6 | async-start | bytes 8388608 | tf_op jit(solution)/shard_map/while
  275.9 5.3 slice-start
  275.9 6.1 %slice-start.1 = ((s8[8388608]{0:T(1024)(128)(4,1)}), s8[4194304]{0:T(1024)(128)(4,1)S(1)}, s32[]{:S(2)}) async-start(s8[8388608]{0:T(1024)(128)(4,1)} %bitcast.218), calls=%async_computation.6 | async-start | bytes 8388608 | tf_op jit(solution)/shard_map/while
  291.7 5.3 slice-start
  291.7 6.1 %slice-start.1 = ((s8[8388608]{0:T(1024)(128)(4,1)}), s8[4194304]{0:T(1024)(128)(4,1)S(1)}, s32[]{:S(2)}) async-start(s8[8388608]{0:T(1024)(128)(4,1)} %bitcast.218), calls=%async_computation.6 | async-start | bytes 8388608 | tf_op jit(solution)/shard_map/while
  307.6 5.3 slice-start
  307.6 6.1 %slice-start.1 = ((s8[8388608]{0:T(1024)(128)(4,1)}), s8[4194304]{0:T(1024)(128)(4,1)S(1)}, s32[]{:S(2)}) async-start(s8[8388608]{0:T(1024)(128)(4,1)} %bitcast.218), calls=%async_computation.6 | async-start | bytes 8388608 | tf_op jit(solution)/shard_map/while
  323.4 5.3 slice-start
  323.4 6.1 %slice-start.1 = ((s8[8388608]{0:T(1024)(128)(4,1)}), s8[4194304]{0:T(1024)(128)(4,1)S(1)}, s32[]{:S(2)}) async-start(s8[8388608]{0:T(1024)(128)(4,1)} %bitcast.218), calls=%async_computation.6 | async-start | bytes 8388608 | tf_op jit(solution)/shard_map/while
  332.2 3.0 copy-start.1
  339.5 3.0 copy-start.1
  347.5 226.5 %reduce-scatter.2.cloned.1.call-start = ((), (), s32[]{:S(2)}) async-start(), calls=%async_computation.4 | async-start | bytes 2359296 | tf_op jit(solution)/shard_map/reduce_scatter | solution.py:137
Sparse Core Ops, SparseCore 0:
  9.2 190.6 all-gather.2
  347.6 175.1 all-gather.4
  530.3 43.7 reduce-scatter.1
